TPU v7x, 32 devices: a whole 2x2x4 slice. The times are simulated.
32 devices in a mesh: groups: 2 (over x), mp: 16 (over z, y, core).
Axes of the slice: x: 2, y: 2, z: 4, core: 2. Of those that a mesh axis runs over, the one named last changes fastest.
Arguments:
- tokens: bfloat16 [512, 8192], P(('groups', 'mp')), parts along dimension 0, may hold values from -6 to 6
- queries: bfloat16 [512, 8192], P(('groups', 'mp')), parts along dimension 0, may hold values from -35 to 35
- key_proj: bfloat16 [512, 1024], P(('groups', 'mp')), parts along dimension 0, may hold values from -5 to 5
- values: bfloat16 [512, 1024], P(('groups', 'mp')), parts along dimension 0, may hold values from -6 to 6
- seq_lens: int32 [12], P('groups'), parts along dimension 0, may hold values from 21 to 85, as said below
- out_weight: bfloat16 [8192, 8192], P('mp'), may hold values from -0.25 to 0.25
- ffn_gain: float32 [2, 8192], replicated, may hold values from 0.25 to 2.5
- gate_weight: bfloat16 [8192, 12288], P(None, 'mp'), may hold values from -0.0625 to 0.0625
- up_weight: bfloat16 [8192, 12288], P(None, 'mp'), may hold values from -0.0625 to 0.0625
- down_weight: bfloat16 [12288, 8192], P('mp'), may hold values from -0.0546875 to 0.0546875
- slice_table: int32 [96], replicated, may hold values from 0 to 1, as said below
Outputs:
- stream: bfloat16 [512, 8192], P(('groups', 'mp')), parts along dimension 0
- mixed: bfloat16 [512, 8192], P(('groups', 'mp')), parts along dimension 0
There are 2 independent parts, one for each index of `groups`. A program takes and returns all parts, laid end to end along the dimension named above; an argument that names none is the same for every part. Nothing has to cross between parts.
Inputs may be any that keep to these rules, and one draw needn't show every extreme that they name: `seq_lens`: the 6 lengths sum to 256; the shortest is exactly 21 and the longest exactly 85. `slice_table`: exactly 16 entries are 1, the rest 0.
All inputs are finite; a program needn't handle non-finite values.
Results may differ from a plain program's by a relative error of at most 0.02.
Values may be sent and summed in bfloat16 or wider, within the bound.
A program may use at most 128 MiB of HBM per device.

v0:
```python
import math
import jax
import jax.numpy as jnp
from jax import lax
from jax.sharding import PartitionSpec as P

QUERY_HEADS = 64
HEAD_SIZE = 128
SLICE = 128


def segment_of(positions, seq_ends):
    return jnp.sum((positions[:, None] >= seq_ends[None, :]).astype(jnp.int32), axis=1)


def allowed(query_pos, key_pos, seq_ends):
    query_seg = segment_of(query_pos, seq_ends)
    key_seg = segment_of(key_pos, seq_ends)
    return (query_seg[:, None] == key_seg[None, :]) & (key_pos[None, :] <= query_pos[:, None])


def soft_weights(scores, visible):
    masked = jnp.where(visible, scores, -1e30)
    highest = jnp.max(masked, axis=-1, keepdims=True)
    expo = jnp.where(visible, jnp.exp(masked - highest), 0.0)
    return (expo / jnp.sum(expo, axis=-1, keepdims=True)).astype(jnp.bfloat16)


def rms_normed(stream_rows):
    stream_full = stream_rows.astype(jnp.float32)
    inv_rms = lax.rsqrt(jnp.mean(stream_full * stream_full, axis=1, keepdims=True) + 1e-05)
    return (stream_full * inv_rms).astype(jnp.bfloat16)


def local(
    tokens,
    queries,
    key_proj,
    values,
    seq_lens,
    out_weight,
    ffn_gain,
    gate_weight,
    up_weight,
    down_weight,
    slice_table,
):
    tok_dev = tokens.shape[0]
    my_index = lax.axis_index("mp")
    token_count = tok_dev * lax.axis_size("mp")
    heads_kv = key_proj.shape[1] // HEAD_SIZE
    query_heads_per_group = QUERY_HEADS // heads_kv
    score_scale = 1.0 / math.sqrt(HEAD_SIZE)
    key_all, value_all = (
        lax.all_gather(key_proj, "mp", axis=0, tiled=True),
        lax.all_gather(values, "mp", axis=0, tiled=True),
    )
    seq_ends = jnp.cumsum(seq_lens)
    key_pos = jnp.arange(token_count, dtype=jnp.int32)
    query_heads = lax.all_to_all(queries, "mp", split_axis=1, concat_axis=0, tiled=True)
    local_heads = query_heads.shape[1] // HEAD_SIZE
    kv_start = my_index * local_heads // query_heads_per_group * HEAD_SIZE
    key_cols = lax.dynamic_slice_in_dim(key_all, kv_start, HEAD_SIZE, 1)
    value_cols = lax.dynamic_slice_in_dim(value_all, kv_start, HEAD_SIZE, 1)
    visible = allowed(key_pos, key_pos, seq_ends)
    scores = (
        jnp.einsum(
            "thd,sd->hts",
            query_heads.reshape(token_count, local_heads, HEAD_SIZE),
            key_cols,
            preferred_element_type=jnp.float32,
        )
        * score_scale
    )
    attn_probs = soft_weights(scores, visible[None])
    context = (
        jnp.einsum("hts,sd->thd", attn_probs, value_cols, preferred_element_type=jnp.float32)
        .astype(jnp.bfloat16)
        .reshape(token_count, local_heads * HEAD_SIZE)
    )
    picked = context
    attn_share = lax.psum_scatter(
        jnp.dot(picked, out_weight, preferred_element_type=jnp.float32).astype(jnp.bfloat16),
        "mp",
        scatter_dimension=0,
        tiled=True,
    ).astype(jnp.float32)
    stream = (tokens.astype(jnp.float32) + attn_share).astype(jnp.bfloat16)
    sent_rows = rms_normed(stream)
    slice_count = gate_weight.shape[1] // SLICE
    row_piece = lax.all_gather(sent_rows, "mp", axis=0, tiled=True)
    outputs = []
    for slice_pos in range(slice_count):
        ffn_which = lax.dynamic_index_in_dim(
            slice_table, my_index * slice_count + slice_pos, 0, keepdims=False
        )
        gain_row = lax.dynamic_index_in_dim(ffn_gain, ffn_which, 0, keepdims=False)
        slice_input = (row_piece.astype(jnp.float32) * gain_row[None, :]).astype(jnp.bfloat16)
        gate_val = jnp.dot(
            slice_input,
            gate_weight[:, slice_pos * SLICE : (slice_pos + 1) * SLICE],
            preferred_element_type=jnp.float32,
        )
        up_val = jnp.dot(
            slice_input,
            up_weight[:, slice_pos * SLICE : (slice_pos + 1) * SLICE],
            preferred_element_type=jnp.float32,
        )
        outputs.append((jax.nn.silu(gate_val) * up_val).astype(jnp.bfloat16))
    hidden = jnp.concatenate(outputs, axis=1)
    picked = hidden
    ffn_share = lax.psum_scatter(
        jnp.dot(picked, down_weight, preferred_element_type=jnp.float32).astype(jnp.bfloat16),
        "mp",
        scatter_dimension=0,
        tiled=True,
    ).astype(jnp.float32)
    mixed = (stream.astype(jnp.float32) + ffn_share).astype(jnp.bfloat16)
    return (stream, mixed)


def solution(mesh):
    placed = (
        P(("groups", "mp"), None),
        P(("groups", "mp"), None),
        P(("groups", "mp"), None),
        P(("groups", "mp"), None),
        P("groups"),
        P("mp", None),
        P(),
        P(None, "mp"),
        P(None, "mp"),
        P("mp", None),
        P(),
    )
    return jax.shard_map(
        local,
        mesh=mesh,
        in_specs=placed,
        out_specs=(P(("groups", "mp"), None), P(("groups", "mp"), None)),
        check_vma=False,
    )
```

profile of v0, /device:TPU:0, one launch (start us, length us, event | category | flops | bytes accessed | tf_op | source)
XLA Modules:
  0.0 304.8 jit_solution(16253626223594990531)
XLA Ops:
  7.2 1.7 copy.43
  8.8 7.4 %all-to-all-start = ((bf16[16,16,512]{2,0,1:T(8,128)(2,1)}), bf16[16,16,512]{2,0,1:T(8,128)(2,1)S(1)}, u32[]{:S(2)}, u32[]{:S(2)}) async-start(bf16[16,16,512]{2,0,1:T(8,128)(2,1)} %bitcast.57), calls=%async_computation | async-start | bytes 524288 | tf_op jit(solution)/shard_map/all_to_all | solution.py:60
  16.2 0.0 reduce-scatter.3.cloned.1.call-start
  16.3 0.8 reduce-window.8
  17.1 0.1 convert_reduce_fusion
  17.2 0.1 fusion.142
  17.3 23.5 %all_gather.10 = bf16[256,1024]{1,0:T(8,128)(2,1)S(1)} all-gather(bf16[16,1024]{1,0:T(8,128)(2,1)} %param.13), channel_id=1, replica_groups=mesh['groups'=2,'mp'=16] {'mp'}, dimensions={0}, use_global_device_ids=true | all-gather | bytes 557056 | tf_op jit(solution)/shard_map/all_gather | solution.py:55
  40.8 19.1 %all_gather.9 = bf16[256,1024]{1,0:T(8,128)(2,1)S(1)} all-gather(bf16[16,1024]{1,0:T(8,128)(2,1)} %param.14), channel_id=1, replica_groups=mesh['groups'=2,'mp'=16] {'mp'}, dimensions={0}, use_global_device_ids=true | all-gather | bytes 557056 | tf_op jit(solution)/shard_map/all_gather | solution.py:56
  59.9 0.0 all-to-all-done
  59.9 0.1 reshape.90
  60.0 0.6 fusion.181
  60.6 0.8 convolution_convert_fusion.2
  61.4 7.7 %convolution_convert_fusion = bf16[256,8192]{1,0:T(8,128)(2,1)} fusion(bf16[256,512]{0,1:T(8,128)(2,1)S(1)} %bitcast.61, bf16[512,8192]{1,0:T(8,128)(2,1)} %param.16), kind=kOutput, calls=%fused_computation.7 | convolution fusion | flops 2149580800 | bytes 12845056 | tf_op jit(solution)/shard_map/dot_general | solution.py:83
  69.1 0.0 reduce-scatter.3.cloned.1.call-update
  69.1 0.0 all-gather.2.cloned.1.call-start
  69.2 70.8 %reduce-scatter.3.cloned.1.call-done = bf16[16,8192]{1,0:T(8,128)(2,1)} async-done(((bf16[256,8192]{1,0:T(8,128)(2,1)}), bf16[16,8192]{1,0:T(8,128)(2,1)}) %reduce-scatter.3.cloned.1.call-update) | async-done | bytes 262160 | tf_op jit(solution)/shard_map/reduce_scatter | solution.py:82
  140.0 1.2 fusion.138
  141.2 0.8 fusion.139
  142.0 0.0 all-gather.2.cloned.1.call-update
  142.1 0.2 reduce-scatter.5.cloned.1.call-start
  142.3 0.7 fusion.180
  154.1 0.2 constant_dynamic-slice_fusion
  154.3 38.4 %all-gather.2.cloned.1.call-done = bf16[256,8192]{1,0:T(8,128)(2,1)} async-done(((bf16[16,8192]{1,0:T(8,128)(2,1)}), bf16[256,8192]{1,0:T(8,128)(2,1)}) %all-gather.2.cloned.1.call-update) | async-done | bytes 4194320 | tf_op jit(solution)/shard_map/all_gather | solution.py:91
  192.6 4.4 %fusion.29 = f32[256,128]{0,1:T(8,128)S(1)} fusion(bf16[256,8192]{1,0:T(8,128)(2,1)} %all-gather.2.cloned.1.call-done, f32[8192]{0:T(1024)S(1)} %bitcast.73, bf16[8192,768]{1,0:T(8,128)(2,1)} %param.18), kind=kOutput, calls=%fused_computation.26 | convolution fusion | flops 543162368 | bytes 6455296 | tf_op jit(solution)/shard_map/dot_general | solution.py:99
  197.1 0.0 slice-start.4
  197.1 3.2 %fusion.25 = f32[256,128]{0,1:T(8,128)S(1)} fusion(bf16[256,8192]{1,0:T(8,128)(2,1)S(1)} %copy-done.4, f32[8192]{0:T(1024)S(1)} %bitcast.71, bf16[8192,768]{1,0:T(8,128)(2,1)} %param.18), kind=kOutput, calls=%fused_computation.24 | convolution fusion | flops 543162368 | bytes 6455296 | tf_op jit(solution)/shard_map/dot_general | solution.py:99
  200.3 0.0 slice-start.5
  200.3 3.2 %fusion.21 = f32[256,128]{0,1:T(8,128)S(1)} fusion(bf16[256,8192]{1,0:T(8,128)(2,1)S(1)} %copy-done.4, f32[8192]{0:T(1024)S(1)} %bitcast.69, bf16[8192,768]{1,0:T(8,128)(2,1)} %param.18), kind=kOutput, calls=%fused_computation.22 | convolution fusion | flops 543162368 | bytes 6455296 | tf_op jit(solution)/shard_map/dot_general | solution.py:99
  203.5 0.0 slice-start.6
  203.5 1.5 fusion.17
  205.0 0.0 slice-start.7
  205.1 1.5 fusion.13
  206.5 0.0 slice-start.8
  206.6 1.5 fusion.9
  208.1 0.9 slice-done.8
  209.0 1.4 fusion.108
  210.4 1.4 fusion.113
  211.8 1.5 fusion.118
  213.3 0.0 slice-start
  213.3 1.6 fusion.123
  214.9 0.5 copy-done.5
  215.5 1.5 fusion.128
  216.9 0.0 slice-start.2
  216.9 3.2 %fusion.133 = bf16[256,768]{0,1:T(8,128)(2,1)S(1)} fusion(bf16[256,768]{0,1:T(8,128)(2,1)S(1)} %fusion.128, bf16[8192,768]{1,0:T(8,128)(2,1)} %param.19, bf16[256,8192]{1,0:T(8,128)(2,1)S(1)} %copy-done.5, f32[8192]{0:T(1024)S(1)} %bitcast.64, f32[256,128]{0,1:T(8,128)S(1)} %fusion.9), kind=kOutput, calls=%fused_computation.63 | convolution fusion | flops 543358976 | bytes 6520832 | tf_op jit(solution)/shard_map/dot_general | solution.py:104
  220.2 5.1 %convolution_convert_fusion.1 = bf16[256,8192]{1,0:T(8,128)(2,1)} fusion(bf16[256,768]{0,1:T(8,128)(2,1)S(1)} %fusion.133, bf16[768,8192]{1,0:T(8,128)(2,1)S(1)} %bitcast.59), kind=kOutput, calls=%fused_computation.8 | convolution fusion | flops 3223322624 | bytes 17170432 | tf_op jit(solution)/shard_map/dot_general | solution.py:113
  225.3 0.0 reduce-scatter.5.cloned.1.call-update
  225.3 71.3 %reduce-scatter.5.cloned.1.call-done = bf16[16,8192]{1,0:T(8,128)(2,1)} async-done(((bf16[256,8192]{1,0:T(8,128)(2,1)}), bf16[16,8192]{1,0:T(8,128)(2,1)}) %reduce-scatter.5.cloned.1.call-update) | async-done | bytes 262160 | tf_op jit(solution)/shard_map/reduce_scatter | solution.py:112
  296.6 1.7 fusion.140
  (25 shorter events, 0.0 us)
Async XLA Ops:
  8.8 51.1 %all-to-all-start = ((bf16[16,16,512]{2,0,1:T(8,128)(2,1)}), bf16[16,16,512]{2,0,1:T(8,128)(2,1)S(1)}, u32[]{:S(2)}, u32[]{:S(2)}) async-start(bf16[16,16,512]{2,0,1:T(8,128)(2,1)} %bitcast.57), calls=%async_computation | async-start | bytes 524288 | tf_op jit(solution)/shard_map/all_to_all | solution.py:60
  16.2 123.8 %reduce-scatter.3.cloned.1.call-start = ((), (), s32[]{:S(2)}) async-start(), calls=%async_computation.3 | async-start | bytes 4456448 | tf_op jit(solution)/shard_map/reduce_scatter | solution.py:82
  69.1 70.9 %copy-start.2 = (bf16[16,8192]{1,0:T(8,128)(2,1)S(1)}, bf16[16,8192]{1,0:T(8,128)(2,1)}, u32[]{:S(2)}) copy-start(bf16[16,8192]{1,0:T(8,128)(2,1)} %param.11) | copy-start | bytes 786436
  69.1 73.2 %copy-start.3 = (s32[96]{0:T(128)S(1)}, s32[96]{0:T(128)}, u32[]{:S(2)}) copy-start(s32[96]{0:T(128)} %param.21) | copy-start | bytes 1156
  69.1 85.0 %copy-start.1 = (f32[2,8192]{1,0:T(2,128)S(1)}, f32[2,8192]{1,0:T(2,128)}, u32[]{:S(2)}) copy-start(f32[2,8192]{1,0:T(2,128)} %param.17) | copy-start | bytes 196612
  69.1 123.5 %all-gather.2.cloned.1.call-start = ((), (), s32[]{:S(2)}) async-start(), calls=%async_computation.4 | async-start | bytes 4456448 | tf_op jit(solution)/shard_map/all_gather | solution.py:91
  141.2 155.4 %copy-start = (bf16[16,8192]{1,0:T(8,128)(2,1)}, bf16[16,8192]{1,0:T(8,128)(2,1)S(1)}, u32[]{:S(2)}) copy-start(bf16[16,8192]{1,0:T(8,128)(2,1)S(1)} %get-tuple-element.3) | copy-start | bytes 786436
  142.1 154.5 %reduce-scatter.5.cloned.1.call-start = ((), (), s32[]{:S(2)}) async-start(), calls=%async_computation.5 | async-start | bytes 4456448 | tf_op jit(solution)/shard_map/reduce_scatter | solution.py:112
  192.6 4.5 %copy-start.4 = (bf16[256,8192]{1,0:T(8,128)(2,1)S(1)}, bf16[256,8192]{1,0:T(8,128)(2,1)}, u32[]{:S(2)}) copy-start(bf16[256,8192]{1,0:T(8,128)(2,1)} %all-gather.2.cloned.1.call-done) | copy-start | bytes 12582916
  192.6 10.8 %slice-start.3 = ((s8[12582912]{0:T(1024)(128)(4,1)}), s8[4194304]{0:T(1024)(128)(4,1)S(1)}, s32[]{:S(2)}) async-start(s8[12582912]{0:T(1024)(128)(4,1)} %bitcast.75), calls=%async_computation.9 | async-start | bytes 8388608
  197.1 6.4 %slice-start.4 = ((s8[12582912]{0:T(1024)(128)(4,1)}), s8[4194304]{0:T(1024)(128)(4,1)S(1)}, s32[]{:S(2)}) async-start(s8[12582912]{0:T(1024)(128)(4,1)} %bitcast.75), calls=%async_computation.10 | async-start | bytes 8388608
  200.3 3.2 %slice-start.5 = ((s8[12582912]{0:T(1024)(128)(4,1)}), s8[4194304]{0:T(1024)(128)(4,1)S(1)}, s32[]{:S(2)}) async-start(s8[12582912]{0:T(1024)(128)(4,1)} %bitcast.75), calls=%async_computation.11 | async-start | bytes 8388608
  203.5 4.6 %slice-start.6 = ((s8[12582912]{0:T(1024)(128)(4,1)}), s8[4194304]{0:T(1024)(128)(4,1)S(1)}, s32[]{:S(2)}) async-start(s8[12582912]{0:T(1024)(128)(4,1)} %bitcast.77), calls=%async_computation.12 | async-start | bytes 8388608
  205.0 3.0 slice-start.7
  206.5 2.4 slice-start.8
  213.3 2.2 copy-start.5
  213.3 6.9 %slice-start = ((s8[12582912]{0:T(1024)(128)(4,1)}), s8[4194304]{0:T(1024)(128)(4,1)S(1)}, s32[]{:S(2)}) async-start(s8[12582912]{0:T(1024)(128)(4,1)} %bitcast.58), calls=%async_computation.6 | async-start | bytes 8388608
  215.5 4.7 %slice-start.1 = ((s8[12582912]{0:T(1024)(128)(4,1)}), s8[4194304]{0:T(1024)(128)(4,1)S(1)}, s32[]{:S(2)}) async-start(s8[12582912]{0:T(1024)(128)(4,1)} %bitcast.58), calls=%async_computation.7 | async-start | bytes 8388608
  216.9 3.3 %slice-start.2 = ((s8[12582912]{0:T(1024)(128)(4,1)}), s8[4194304]{0:T(1024)(128)(4,1)S(1)}, s32[]{:S(2)}) async-start(s8[12582912]{0:T(1024)(128)(4,1)} %bitcast.58), calls=%async_computation.8 | async-start | bytes 8388608
Sparse Core Ops, SparseCore 0:
  69.2 70.7 reduce-scatter.2
  143.0 49.6 all-gather.1
  225.4 71.1 reduce-scatter.4
where the time goes:
time: 305 us
  waiting for transfers between devices  181 us (59%)
  blocking collectives  42.6 us (14%)
  matrix products  40 us (13%)
  between operations  25.2 us (8%)
  starting transfers between devices  7.69 us (3%)
  other arithmetic  4.74 us (2%)
  local copies, waits for them, and re-layouts  4.1 us (1%)
    reduce_scatter x1, waiting for transfers between devices, local(): lax.psum_scatter(jnp.dot(picked, down_weight, preferred_element_type=jnp....  71.3 us
    reduce_scatter x1, waiting for transfers between devices, local(): lax.psum_scatter(jnp.dot(picked, out_weight, preferred_element_type=jnp.f...  70.8 us
    all_gather x1, waiting for transfers between devices, local(): row_piece = lax.all_gather(sent_rows, 'mp', axis=0, tiled=True)  38.4 us
    all_gather x1, blocking collectives, local(): lax.all_gather(key_proj, 'mp', axis=0, tiled=True)  23.5 us
    all_gather x1, blocking collectives, local(): lax.all_gather(values, 'mp', axis=0, tiled=True)  19.1 us
    dot_general x6, matrix products, local(): jnp.dot(slice_input, gate_weight[:, slice_pos * SLICE:(slice_pos + 1) * S...  15.3 us
    dot_general x6, matrix products, local(): jnp.dot(slice_input, up_weight[:, slice_pos * SLICE:(slice_pos + 1) * SLI...  10.6 us
    dot_general x1, matrix products, local(): jnp.dot(picked, out_weight, preferred_element_type=jnp.float32)  7.71 us
  transfers between devices with their start and end apart: 4, of which 3 were waited for; matrix products, arithmetic and copies ran while one was open for 1% of the time, Pallas kernels for 0%

commit v1 on v0

--- a/solution.py
+++ b/solution.py
@@ -57,7 +57,10 @@
     )
     seq_ends = jnp.cumsum(seq_lens)
     key_pos = jnp.arange(token_count, dtype=jnp.int32)
-    query_heads = lax.all_to_all(queries, "mp", split_axis=1, concat_axis=0, tiled=True)
+    query_heads = jnp.concatenate(
+        lax.all_to_all(jnp.stack(jnp.split(queries, lax.axis_size("mp"), axis=1)), "mp", 0, 0),
+        axis=0,
+    )
     local_heads = query_heads.shape[1] // HEAD_SIZE
     kv_start = my_index * local_heads // query_heads_per_group * HEAD_SIZE
     key_cols = lax.dynamic_slice_in_dim(key_all, kv_start, HEAD_SIZE, 1)

time: 305 us -> 326 us (1.069)
  local copies, waits for them, and re-layouts: 4.1 us -> 23.6 us
    unnamed x30 -> x45, local copies, waits for them, and re-layouts: 1.48 us -> 21.3 us
where the time goes in v1:
time: 326 us; the launch traced here: 324 us
  waiting for transfers between devices  180 us (55%)
  blocking collectives  42.6 us (13%)
  matrix products  40 us (12%)
  between operations  25.2 us (8%)
  local copies, waits for them, and re-layouts  23.6 us (7%)
  starting transfers between devices  7.69 us (2%)
  other arithmetic  4.74 us (1%)
    reduce_scatter x1, waiting for transfers between devices, local(): lax.psum_scatter(jnp.dot(picked, down_weight, preferred_element_type=jnp....  71.1 us
    reduce_scatter x1, waiting for transfers between devices, local(): lax.psum_scatter(jnp.dot(picked, out_weight, preferred_element_type=jnp.f...  71 us
    all_gather x1, waiting for transfers between devices, local(): row_piece = lax.all_gather(sent_rows, 'mp', axis=0, tiled=True)  38.3 us
    all_gather x1, blocking collectives, local(): lax.all_gather(key_proj, 'mp', axis=0, tiled=True)  23.5 us
    unnamed x45, local copies, waits for them, and re-layouts  21.3 us
    all_gather x1, blocking collectives, local(): lax.all_gather(values, 'mp', axis=0, tiled=True)  19.1 us
    dot_general x6, matrix products, local(): jnp.dot(slice_input, gate_weight[:, slice_pos * SLICE:(slice_pos + 1) * S...  15.3 us
    dot_general x6, matrix products, local(): jnp.dot(slice_input, up_weight[:, slice_pos * SLICE:(slice_pos + 1) * SLI...  10.6 us
  transfers between devices with their start and end apart: 4, of which 3 were waited for; matrix products, arithmetic and copies ran while one was open for 1% of the time, Pallas kernels for 0%

profile of v1, /device:TPU:0, one launch (start us, length us, event | category | flops | bytes accessed | tf_op | source)
XLA Modules:
  0.0 324.1 jit_solution(379861838894190509)
XLA Ops:
  7.2 1.3 constant_dynamic-update-slice_fusion.15
  8.5 1.3 constant_dynamic-update-slice_fusion.14
  9.8 1.3 constant_dynamic-update-slice_fusion.13
  11.1 1.3 constant_dynamic-update-slice_fusion.12
  12.5 1.3 constant_dynamic-update-slice_fusion.11
  13.8 1.3 constant_dynamic-update-slice_fusion.10
  15.1 1.3 constant_dynamic-update-slice_fusion.9
  16.4 1.3 constant_dynamic-update-slice_fusion.8
  17.8 1.3 constant_dynamic-update-slice_fusion.7
  19.1 1.3 constant_dynamic-update-slice_fusion.6
  20.4 1.3 constant_dynamic-update-slice_fusion.5
  21.7 1.3 constant_dynamic-update-slice_fusion.4
  23.0 1.3 constant_dynamic-update-slice_fusion.3
  24.4 1.3 constant_dynamic-update-slice_fusion.2
  25.7 1.3 constant_dynamic-update-slice_fusion.1
  27.0 1.3 constant_dynamic-update-slice_fusion
  28.3 7.4 %all-to-all-start = ((bf16[16,16,512]{2,1,0:T(8,128)(2,1)}), bf16[16,16,512]{2,1,0:T(8,128)(2,1)S(1)}, u32[]{:S(2)}, u32[]{:S(2)}) async-start(bf16[16,16,512]{2,1,0:T(8,128)(2,1)} %constant_dynamic-update-slice_fusion), calls=%async_computation | async-start | bytes 524288 | tf_op jit(solution)/shard_map/all_to_all | solution.py:61
  35.8 0.8 reduce-window.8
  36.7 0.1 fusion.142
  36.8 23.5 %all_gather.10 = bf16[256,1024]{1,0:T(8,128)(2,1)S(1)} all-gather(bf16[16,1024]{1,0:T(8,128)(2,1)} %param.13), channel_id=1, replica_groups=mesh['groups'=2,'mp'=16] {'mp'}, dimensions={0}, use_global_device_ids=true | all-gather | bytes 557056 | tf_op jit(solution)/shard_map/all_gather | solution.py:55
  60.3 19.1 %all_gather.9 = bf16[256,1024]{1,0:T(8,128)(2,1)S(1)} all-gather(bf16[16,1024]{1,0:T(8,128)(2,1)} %param.14), channel_id=1, replica_groups=mesh['groups'=2,'mp'=16] {'mp'}, dimensions={0}, use_global_device_ids=true | all-gather | bytes 557056 | tf_op jit(solution)/shard_map/all_gather | solution.py:56
  79.5 0.6 fusion.181
  80.1 0.8 convolution_convert_fusion.2
  80.9 7.7 %convolution_convert_fusion = bf16[256,8192]{1,0:T(8,128)(2,1)} fusion(bf16[256,512]{0,1:T(8,128)(2,1)S(1)} %bitcast.87, bf16[512,8192]{1,0:T(8,128)(2,1)} %param.16), kind=kOutput, calls=%fused_computation.7 | convolution fusion | flops 2149580800 | bytes 12845056 | tf_op jit(solution)/shard_map/dot_general | solution.py:86
  88.7 71.0 %reduce-scatter.3.cloned.1.call-done = bf16[16,8192]{1,0:T(8,128)(2,1)} async-done(((bf16[256,8192]{1,0:T(8,128)(2,1)}), bf16[16,8192]{1,0:T(8,128)(2,1)}) %reduce-scatter.3.cloned.1.call-update) | async-done | bytes 262160 | tf_op jit(solution)/shard_map/reduce_scatter | solution.py:85
  159.6 1.2 fusion.138
  160.8 0.8 fusion.139
  161.7 0.2 reduce-scatter.5.cloned.1.call-start
  161.9 0.7 fusion.180
  173.7 0.2 constant_dynamic-slice_fusion
  173.9 38.3 %all-gather.2.cloned.1.call-done = bf16[256,8192]{1,0:T(8,128)(2,1)} async-done(((bf16[16,8192]{1,0:T(8,128)(2,1)}), bf16[256,8192]{1,0:T(8,128)(2,1)}) %all-gather.2.cloned.1.call-update) | async-done | bytes 4194320 | tf_op jit(solution)/shard_map/all_gather | solution.py:94
  212.2 4.4 %fusion.29 = f32[256,128]{0,1:T(8,128)S(1)} fusion(bf16[256,8192]{1,0:T(8,128)(2,1)} %all-gather.2.cloned.1.call-done, f32[8192]{0:T(1024)S(1)} %bitcast.98, bf16[8192,768]{1,0:T(8,128)(2,1)} %param.18), kind=kOutput, calls=%fused_computation.26 | convolution fusion | flops 543162368 | bytes 6455296 | tf_op jit(solution)/shard_map/dot_general | solution.py:102
  216.6 3.2 fusion.25
  219.8 3.2 fusion.21
  223.0 1.5 fusion.17
  224.6 1.5 fusion.13
  226.1 1.5 fusion.9
  227.6 0.9 slice-done.8
  228.5 1.4 fusion.108
  229.9 1.4 fusion.113
  231.3 1.5 fusion.118
  232.8 1.6 fusion.123
  234.4 0.5 copy-done.5
  235.0 1.5 fusion.128
  236.5 3.2 fusion.133
  239.7 5.1 %convolution_convert_fusion.1 = bf16[256,8192]{1,0:T(8,128)(2,1)} fusion(bf16[256,768]{0,1:T(8,128)(2,1)S(1)} %fusion.133, bf16[768,8192]{1,0:T(8,128)(2,1)S(1)} %bitcast.86), kind=kOutput, calls=%fused_computation.8 | convolution fusion | flops 3223322624 | bytes 17170432 | tf_op jit(solution)/shard_map/dot_general | solution.py:116
  244.8 71.1 %reduce-scatter.5.cloned.1.call-done = bf16[16,8192]{1,0:T(8,128)(2,1)} async-done(((bf16[256,8192]{1,0:T(8,128)(2,1)}), bf16[16,8192]{1,0:T(8,128)(2,1)}) %reduce-scatter.5.cloned.1.call-update) | async-done | bytes 262160 | tf_op jit(solution)/shard_map/reduce_scatter | solution.py:115
  315.9 1.7 fusion.140
  (40 shorter events, 0.4 us)
Async XLA Ops:
  28.3 51.1 %all-to-all-start = ((bf16[16,16,512]{2,1,0:T(8,128)(2,1)}), bf16[16,16,512]{2,1,0:T(8,128)(2,1)S(1)}, u32[]{:S(2)}, u32[]{:S(2)}) async-start(bf16[16,16,512]{2,1,0:T(8,128)(2,1)} %constant_dynamic-update-slice_fusion), calls=%async_computation | async-start | bytes 524288 | tf_op jit(solution)/shard_map/all_to_all | solution.py:61
  35.7 123.9 %reduce-scatter.3.cloned.1.call-start = ((), (), s32[]{:S(2)}) async-start(), calls=%async_computation.3 | async-start | bytes 4456448 | tf_op jit(solution)/shard_map/reduce_scatter | solution.py:85
  88.6 71.0 %copy-start.2 = (bf16[16,8192]{1,0:T(8,128)(2,1)S(1)}, bf16[16,8192]{1,0:T(8,128)(2,1)}, u32[]{:S(2)}) copy-start(bf16[16,8192]{1,0:T(8,128)(2,1)} %param.11) | copy-start | bytes 786436
  88.6 73.3 %copy-start.3 = (s32[96]{0:T(128)S(1)}, s32[96]{0:T(128)}, u32[]{:S(2)}) copy-start(s32[96]{0:T(128)} %param.21) | copy-start | bytes 1156
  88.6 85.1 %copy-start.1 = (f32[2,8192]{1,0:T(2,128)S(1)}, f32[2,8192]{1,0:T(2,128)}, u32[]{:S(2)}) copy-start(f32[2,8192]{1,0:T(2,128)} %param.17) | copy-start | bytes 196612
  88.6 123.6 %all-gather.2.cloned.1.call-start = ((), (), s32[]{:S(2)}) async-start(), calls=%async_computation.4 | async-start | bytes 4456448 | tf_op jit(solution)/shard_map/all_gather | solution.py:94
  160.8 155.1 %copy-start = (bf16[16,8192]{1,0:T(8,128)(2,1)}, bf16[16,8192]{1,0:T(8,128)(2,1)S(1)}, u32[]{:S(2)}) copy-start(bf16[16,8192]{1,0:T(8,128)(2,1)S(1)} %get-tuple-element.3) | copy-start | bytes 786436
  161.7 154.2 %reduce-scatter.5.cloned.1.call-start = ((), (), s32[]{:S(2)}) async-start(), calls=%async_computation.5 | async-start | bytes 4456448 | tf_op jit(solution)/shard_map/reduce_scatter | solution.py:115
  212.2 4.4 %copy-start.4 = (bf16[256,8192]{1,0:T(8,128)(2,1)S(1)}, bf16[256,8192]{1,0:T(8,128)(2,1)}, u32[]{:S(2)}) copy-start(bf16[256,8192]{1,0:T(8,128)(2,1)} %all-gather.2.cloned.1.call-done) | copy-start | bytes 12582916
  212.2 10.8 %slice-start.3 = ((s8[12582912]{0:T(1024)(128)(4,1)}), s8[4194304]{0:T(1024)(128)(4,1)S(1)}, s32[]{:S(2)}) async-start(s8[12582912]{0:T(1024)(128)(4,1)} %bitcast.100), calls=%async_computation.9 | async-start | bytes 8388608
  216.6 6.4 %slice-start.4 = ((s8[12582912]{0:T(1024)(128)(4,1)}), s8[4194304]{0:T(1024)(128)(4,1)S(1)}, s32[]{:S(2)}) async-start(s8[12582912]{0:T(1024)(128)(4,1)} %bitcast.100), calls=%async_computation.10 | async-start | bytes 8388608
  219.8 3.2 slice-start.5
  223.0 4.6 %slice-start.6 = ((s8[12582912]{0:T(1024)(128)(4,1)}), s8[4194304]{0:T(1024)(128)(4,1)S(1)}, s32[]{:S(2)}) async-start(s8[12582912]{0:T(1024)(128)(4,1)} %bitcast.102), calls=%async_computation.12 | async-start | bytes 8388608
  224.6 3.0 slice-start.7
  226.1 2.4 slice-start.8
  232.8 2.2 copy-start.5
  232.8 6.9 %slice-start = ((s8[12582912]{0:T(1024)(128)(4,1)}), s8[4194304]{0:T(1024)(128)(4,1)S(1)}, s32[]{:S(2)}) async-start(s8[12582912]{0:T(1024)(128)(4,1)} %bitcast.85), calls=%async_computation.6 | async-start | bytes 8388608
  235.0 4.7 %slice-start.1 = ((s8[12582912]{0:T(1024)(128)(4,1)}), s8[4194304]{0:T(1024)(128)(4,1)S(1)}, s32[]{:S(2)}) async-start(s8[12582912]{0:T(1024)(128)(4,1)} %bitcast.85), calls=%async_computation.7 | async-start | bytes 8388608
  236.4 3.3 %slice-start.2 = ((s8[12582912]{0:T(1024)(128)(4,1)}), s8[4194304]{0:T(1024)(128)(4,1)S(1)}, s32[]{:S(2)}) async-start(s8[12582912]{0:T(1024)(128)(4,1)} %bitcast.85), calls=%async_computation.8 | async-start | bytes 8388608
Sparse Core Ops, SparseCore 0:
  88.7 70.8 reduce-scatter.2
  162.6 49.5 all-gather.1
  245.0 70.8 reduce-scatter.4
